TPU v7x, 32 devices: a whole 2x2x4 slice. The times are simulated.
32 devices in a mesh: enc: 4 (over z), dp: 8 (over y, x, core).
Axes of the slice: x: 2, y: 2, z: 4, core: 2. Of those that a mesh axis runs over, the one named last changes fastest.
Arguments:
- text: bfloat16 [16384, 768], P(('enc', 'dp')), may hold values from -6 to 6
- region_feats: bfloat16 [13312, 2048], P(('enc', 'dp')), may hold values from -6 to 6
- boxes: bfloat16 [4, 13312], P(None, ('enc', 'dp')), may hold values from 0 to 1
- caption_count: int32 [128], P(('enc', 'dp')), may hold values from 8 to 128, as said below
- region_count: int32 [128], P(('enc', 'dp')), may hold values from 36 to 100, as said below
- region_offset: int32 [32], P(('enc', 'dp')), may hold values from 0 to 31
- w_img: bfloat16 [2048, 768], P(('enc', 'dp')), may hold values from -0.125 to 0.125
- w_box: bfloat16 [4, 768], replicated, may hold values from -3 to 3
- b_img: float32 [768], replicated, may hold values from -3 to 3
- g_reg: float32 [768], replicated, may hold values from 0.25 to 1.75
- beta_reg: float32 [768], replicated, may hold values from -1.75 to 1.75
- w_query: bfloat16 [768, 768], P(('enc', 'dp')), may hold values from -0.21875 to 0.21875
- b_query: float32 [768], replicated, may hold values from -1.75 to 1.75
- w_key: bfloat16 [768, 768], P(('enc', 'dp')), may hold values from -0.21875 to 0.21875
- w_value: bfloat16 [768, 768], P(('enc', 'dp')), may hold values from -0.21875 to 0.21875
- b_value: float32 [768], replicated, may hold values from -1.75 to 1.75
- w_out: bfloat16 [768, 768], P(('enc', 'dp')), may hold values from -1.75 to 1.75
- b_out: float32 [768], replicated, may hold values from -1.75 to 1.75
- g_one: float32 [768], replicated, may hold values from 0.25 to 1.75
- beta_one: float32 [768], replicated, may hold values from -1.75 to 1.75
- w_up: bfloat16 [768, 3072], P(('enc', 'dp')), may hold values from -0.21875 to 0.21875
- b_up: float32 [3072], replicated, may hold values from -1.75 to 1.75
- w_down: bfloat16 [3072, 768], P(('enc', 'dp')), may hold values from -0.109375 to 0.109375
- b_down: float32 [768], replicated, may hold values from -1.75 to 1.75
- g_two: float32 [768], replicated, may hold values from 0.25 to 1.75
- beta_two: float32 [768], replicated, may hold values from -1.75 to 1.75
- cotangent: bfloat16 [32768, 768], P(('enc', 'dp'))
Outputs:
- output: bfloat16 [32768, 768], P(('enc', 'dp'))
- grad_text: bfloat16 [16384, 768], P(('enc', 'dp'))
- grad_feats: bfloat16 [13312, 2048], P(('enc', 'dp'))
- grad_boxes: bfloat16 [4, 13312], P(None, ('enc', 'dp'))
- grad_w_img: float32 [2048, 768], replicated
- grad_w_box: float32 [4, 768], replicated
- grad_b_img: float32 [768], replicated
- grad_g_reg: float32 [768], replicated
- grad_beta_reg: float32 [768], replicated
- grad_w_query: float32 [768, 768], replicated
- grad_b_query: float32 [768], replicated
- grad_w_key: float32 [768, 768], replicated
- grad_w_value: float32 [768, 768], replicated
- grad_b_value: float32 [768], replicated
- grad_w_out: float32 [768, 768], replicated
- grad_b_out: float32 [768], replicated
- grad_g_one: float32 [768], replicated
- grad_beta_one: float32 [768], replicated
- grad_w_up: float32 [768, 3072], replicated
- grad_b_up: float32 [3072], replicated
- grad_w_down: float32 [3072, 768], replicated
- grad_b_down: float32 [768], replicated
- grad_g_two: float32 [768], replicated
- grad_beta_two: float32 [768], replicated
Inputs may be any that keep to these rules, and one draw needn't show every extreme that they name: `caption_count`: some sequence has exactly 128 caption tokens. `region_count`: in every draw some holder's 4 sequences all have 100 regions.
All inputs are finite; a program needn't handle non-finite values.
Results may differ from a plain program's by a relative error of at most 0.018.
Values may be sent and summed in bfloat16 or wider, within the bound.
No kernel may reach another device: no remote copies, remote signals or barrier semaphores. Data moves between devices by JAX's collectives and lax.ppermute only.
A program may use at most 192 MiB of HBM per device.

v0:
```python
import jax
import jax.numpy as jnp
from jax import lax
from jax.sharding import PartitionSpec as P

HEADS = 12
epsilon = 1e-05


def normalize(values, gain_vec, shift_vec):
    centered = values - jnp.mean(values, -1, keepdims=True)
    inverse = lax.rsqrt(jnp.mean(centered * centered, -1, keepdims=True) + epsilon)
    normed = centered * inverse
    return (normed * gain_vec + shift_vec, normed, inverse)


def normalize_back(upstream, normed, inverse, gain_vec):
    weighted = upstream * gain_vec
    result = inverse * (
        weighted
        - jnp.mean(weighted, -1, keepdims=True)
        - normed * jnp.mean(weighted * normed, -1, keepdims=True)
    )
    return (result, jnp.sum(upstream * normed, 0), jnp.sum(upstream, 0))


def exact_gelu(values):
    return jax.nn.gelu(values, approximate=False)


def outer_sum(row_data, row_grad):
    return jnp.einsum("ra,rb->ab", row_data, row_grad, preferred_element_type=jnp.float32)


def back_product(row_grad, weight):
    return jnp.einsum("rb,ab->ra", row_grad, weight, preferred_element_type=jnp.float32)


def column_sum(row_grad):
    return jnp.sum(row_grad.astype(jnp.float32), 0)


def body(
    text,
    region_feats,
    boxes,
    caption_count,
    region_count,
    region_offset,
    w_img,
    w_box,
    b_img,
    g_reg,
    beta_reg,
    w_query,
    b_query,
    w_key,
    w_value,
    b_value,
    w_out,
    b_out,
    g_one,
    beta_one,
    w_up,
    b_up,
    w_down,
    b_down,
    g_two,
    beta_two,
    cotangent,
):
    img_full, query_full, key_full, value_full, out_full, up_full, down_full = (
        lax.all_gather(w_img, ("enc", "dp"), axis=0, tiled=True),
        lax.all_gather(w_query, ("enc", "dp"), axis=0, tiled=True),
        lax.all_gather(w_key, ("enc", "dp"), axis=0, tiled=True),
        lax.all_gather(w_value, ("enc", "dp"), axis=0, tiled=True),
        lax.all_gather(w_out, ("enc", "dp"), axis=0, tiled=True),
        lax.all_gather(w_up, ("enc", "dp"), axis=0, tiled=True),
        lax.all_gather(w_down, ("enc", "dp"), axis=0, tiled=True),
    )
    device_count = lax.axis_size(("enc", "dp"))
    seq_count = caption_count.shape[0]
    model_width = text.shape[1]
    text_len = text.shape[0] // seq_count
    seq_len = cotangent.shape[0] // seq_count
    region_len = seq_len - text_len
    sent_rows = region_feats.shape[0]
    per_peer = sent_rows // device_count
    head_dim = model_width // HEADS
    score_scale = head_dim ** (-0.5)
    pre_norm = (
        jnp.dot(region_feats, img_full, preferred_element_type=jnp.float32)
        + jnp.einsum("cr,cd->rd", boxes, w_box, preferred_element_type=jnp.float32)
        + b_img
    )
    encoded, enc_normed, enc_inverse = normalize(pre_norm, g_reg, beta_reg)
    received = lax.all_to_all(
        encoded.astype(jnp.bfloat16), ("enc", "dp"), split_axis=0, concat_axis=0, tiled=True
    )
    position = jnp.arange(sent_rows, dtype=jnp.int32)
    arrival = (
        position % per_peer * device_count
        + (position // per_peer - region_offset[0]) % device_count
    )
    starts = jnp.cumsum(region_count) - region_count
    slot_total = seq_count * region_len
    slot_pos = jnp.arange(slot_total, dtype=jnp.int32) % region_len
    wanted = jnp.repeat(starts, region_len, total_repeat_length=slot_total) + slot_pos
    slot_live = slot_pos < jnp.repeat(region_count, region_len, total_repeat_length=slot_total)
    placement = ((wanted[:, None] == arrival[None, :]) & slot_live[:, None]).astype(jnp.bfloat16)
    regions = jnp.dot(placement, received, preferred_element_type=jnp.float32).astype(jnp.bfloat16)
    hidden_in = jnp.concatenate(
        [
            text.reshape(seq_count, text_len, model_width),
            regions.reshape(seq_count, region_len, model_width),
        ],
        1,
    ).reshape(seq_count * seq_len, model_width)
    key_live = jnp.concatenate(
        [
            jnp.arange(text_len)[None, :] < caption_count[:, None],
            jnp.arange(region_len)[None, :] < region_count[:, None],
        ],
        1,
    )
    row_live = key_live.reshape(-1, 1).astype(jnp.float32)

    def heads_view(tensor):
        return tensor.reshape(seq_count, seq_len, HEADS, head_dim)

    query_heads = heads_view(
        (jnp.dot(hidden_in, query_full, preferred_element_type=jnp.float32) + b_query).astype(
            jnp.bfloat16
        )
    )
    key_heads = heads_view(
        jnp.dot(hidden_in, key_full, preferred_element_type=jnp.float32).astype(jnp.bfloat16)
    )
    value_heads = heads_view(
        (jnp.dot(hidden_in, value_full, preferred_element_type=jnp.float32) + b_value).astype(
            jnp.bfloat16
        )
    )
    scores = (
        jnp.einsum("sqhd,skhd->shqk", query_heads, key_heads, preferred_element_type=jnp.float32)
        * score_scale
    )
    scores = jnp.where(key_live[:, None, None, :], scores, -1e30)
    row_max = jnp.max(scores, -1, keepdims=True)
    exp_scores = jnp.exp(scores - row_max)
    attn_probs = exp_scores / jnp.sum(exp_scores, -1, keepdims=True)
    probs_low = attn_probs.astype(jnp.bfloat16)
    context = (
        jnp.einsum("shqk,skhd->sqhd", probs_low, value_heads, preferred_element_type=jnp.float32)
        .reshape(-1, model_width)
        .astype(jnp.bfloat16)
    )
    mixed = (
        hidden_in.astype(jnp.float32)
        + jnp.dot(context, out_full, preferred_element_type=jnp.float32)
        + b_out
    )
    normed_one, one_normed, one_inverse = normalize(mixed, g_one, beta_one)
    normed_one = normed_one.astype(jnp.bfloat16)
    gate_in = jnp.dot(normed_one, up_full, preferred_element_type=jnp.float32) + b_up
    activated = exact_gelu(gate_in).astype(jnp.bfloat16)
    second_in = (
        normed_one.astype(jnp.float32)
        + jnp.dot(activated, down_full, preferred_element_type=jnp.float32)
        + b_down
    )
    normed_two, two_normed, two_inverse = normalize(second_in, g_two, beta_two)
    output = (normed_two * row_live).astype(jnp.bfloat16)
    grad_second = cotangent.astype(jnp.float32) * row_live
    grad_second_in, grad_g_two, grad_beta_two = normalize_back(
        grad_second, two_normed, two_inverse, g_two
    )
    grad_down_out = grad_second_in.astype(jnp.bfloat16)
    grad_w_down = outer_sum(activated, grad_down_out)
    grad_b_down = column_sum(grad_down_out)
    grad_activated = back_product(grad_down_out, down_full)
    gelu_pull = jax.vjp(exact_gelu, gate_in)[1]
    grad_gate = gelu_pull(grad_activated)[0].astype(jnp.bfloat16)
    grad_w_up = outer_sum(normed_one, grad_gate)
    grad_b_up = column_sum(grad_gate)
    grad_first = back_product(grad_gate, up_full) + grad_second_in
    grad_mixed, grad_g_one, grad_beta_one = normalize_back(
        grad_first, one_normed, one_inverse, g_one
    )
    grad_attn = grad_mixed.astype(jnp.bfloat16)
    grad_w_out = outer_sum(context, grad_attn)
    grad_b_out = column_sum(grad_attn)
    grad_context = heads_view(back_product(grad_attn, out_full).astype(jnp.bfloat16))
    grad_probs = jnp.einsum(
        "sqhd,skhd->shqk", grad_context, value_heads, preferred_element_type=jnp.float32
    )
    grad_values = (
        jnp.einsum("shqk,sqhd->skhd", probs_low, grad_context, preferred_element_type=jnp.float32)
        .reshape(-1, model_width)
        .astype(jnp.bfloat16)
    )
    grad_scores = (
        attn_probs * (grad_probs - jnp.sum(attn_probs * grad_probs, -1, keepdims=True))
    ).astype(jnp.bfloat16)
    grad_query = (
        (
            jnp.einsum(
                "shqk,skhd->sqhd", grad_scores, key_heads, preferred_element_type=jnp.float32
            )
            * score_scale
        )
        .reshape(-1, model_width)
        .astype(jnp.bfloat16)
    )
    grad_keys = (
        (
            jnp.einsum(
                "shqk,sqhd->skhd", grad_scores, query_heads, preferred_element_type=jnp.float32
            )
            * score_scale
        )
        .reshape(-1, model_width)
        .astype(jnp.bfloat16)
    )
    grad_w_query = outer_sum(hidden_in, grad_query)
    grad_b_query = column_sum(grad_query)
    grad_w_key = outer_sum(hidden_in, grad_keys)
    grad_w_value = outer_sum(hidden_in, grad_values)
    grad_b_value = column_sum(grad_values)
    grad_hidden = (
        grad_mixed
        + back_product(grad_query, query_full)
        + back_product(grad_keys, key_full)
        + back_product(grad_values, value_full)
    )
    grad_hidden = grad_hidden.reshape(seq_count, seq_len, model_width)
    grad_text = grad_hidden[:, :text_len].reshape(-1, model_width).astype(jnp.bfloat16)
    grad_slots = grad_hidden[:, text_len:].reshape(-1, model_width).astype(jnp.bfloat16)
    grad_sent = jnp.einsum(
        "tn,td->nd", placement, grad_slots, preferred_element_type=jnp.float32
    ).astype(jnp.bfloat16)
    grad_encoded = lax.all_to_all(
        grad_sent, ("enc", "dp"), split_axis=0, concat_axis=0, tiled=True
    ).astype(jnp.float32)
    grad_pre, grad_g_reg, grad_beta_reg = normalize_back(
        grad_encoded, enc_normed, enc_inverse, g_reg
    )
    grad_pre = grad_pre.astype(jnp.bfloat16)
    grad_w_img = outer_sum(region_feats, grad_pre)
    grad_w_box = jnp.einsum("cr,rd->cd", boxes, grad_pre, preferred_element_type=jnp.float32)
    grad_b_img = column_sum(grad_pre)
    grad_feats = back_product(grad_pre, img_full).astype(jnp.bfloat16)
    grad_boxes = jnp.einsum(
        "cd,rd->cr", w_box, grad_pre, preferred_element_type=jnp.float32
    ).astype(jnp.bfloat16)
    (
        grad_w_img,
        grad_w_box,
        grad_b_img,
        grad_g_reg,
        grad_beta_reg,
        grad_w_query,
        grad_b_query,
        grad_w_key,
        grad_w_value,
        grad_b_value,
        grad_w_out,
        grad_b_out,
        grad_g_one,
        grad_beta_one,
        grad_w_up,
        grad_b_up,
        grad_w_down,
        grad_b_down,
        grad_g_two,
        grad_beta_two,
    ) = lax.psum(
        (
            grad_w_img,
            grad_w_box,
            grad_b_img,
            grad_g_reg,
            grad_beta_reg,
            grad_w_query,
            grad_b_query,
            grad_w_key,
            grad_w_value,
            grad_b_value,
            grad_w_out,
            grad_b_out,
            grad_g_one,
            grad_beta_one,
            grad_w_up,
            grad_b_up,
            grad_w_down,
            grad_b_down,
            grad_g_two,
            grad_beta_two,
        ),
        ("enc", "dp"),
    )
    return (
        output,
        grad_text,
        grad_feats,
        grad_boxes,
        grad_w_img,
        grad_w_box,
        grad_b_img,
        grad_g_reg,
        grad_beta_reg,
        grad_w_query,
        grad_b_query,
        grad_w_key,
        grad_w_value,
        grad_b_value,
        grad_w_out,
        grad_b_out,
        grad_g_one,
        grad_beta_one,
        grad_w_up,
        grad_b_up,
        grad_w_down,
        grad_b_down,
        grad_g_two,
        grad_beta_two,
    )


def solution(mesh):
    return jax.shard_map(
        body,
        mesh=mesh,
        in_specs=(
            P(("enc", "dp"), None),
            P(("enc", "dp"), None),
            P(None, ("enc", "dp")),
            P(("enc", "dp")),
            P(("enc", "dp")),
            P(("enc", "dp")),
            P(("enc", "dp"), None),
            P(),
            P(),
            P(),
            P(),
            P(("enc", "dp"), None),
            P(),
            P(("enc", "dp"), None),
            P(("enc", "dp"), None),
            P(),
            P(("enc", "dp"), None),
            P(),
            P(),
            P(),
            P(("enc", "dp"), None),
            P(),
            P(("enc", "dp"), None),
            P(),
            P(),
            P(),
            P(("enc", "dp"), None),
        ),
        out_specs=(
            P(("enc", "dp"), None),
            P(("enc", "dp"), None),
            P(("enc", "dp"), None),
            P(None, ("enc", "dp")),
            P(),
            P(),
            P(),
            P(),
            P(),
            P(),
            P(),
            P(),
            P(),
            P(),
            P(),
            P(),
            P(),
            P(),
            P(),
            P(),
            P(),
            P(),
            P(),
            P(),
        ),
        check_vma=False,
    )
```

profile of v0, /device:TPU:0, one launch (start us, length us, event | category | flops | bytes accessed | tf_op | source)
XLA Modules:
  0.0 1141.4 jit_solution(5793821062588575223)
XLA Ops:
  11.2 61.4 %all-gather.8.cloned.1.call-done = bf16[2048,768]{1,0:T(8,128)(2,1)} async-done(((bf16[64,768]{1,0:T(8,128)(2,1)}), bf16[2048,768]{1,0:T(8,128)(2,1)}) %all-gather.8.cloned.1.call-update) | async-done | bytes 3145744 | tf_op jit(solution)/shard_map/all_gather | solution.py:73
  72.6 3.4 fusion.82
  79.5 3.4 all-to-all-start
  85.8 2.6 select_compare_fusion
  89.0 2.6 select_add_fusion
  91.7 12.7 %all-to-all-done = bf16[32,13,768]{2,1,0:T(8,128)(2,1)S(1)} async-done(((bf16[32,13,768]{2,1,0:T(8,128)(2,1)}), bf16[32,13,768]{2,1,0:T(8,128)(2,1)S(1)}, u32[]{:S(2)}, u32[]{:S(2)}) %all-to-all-start) | async-done | bytes 639008 | tf_op jit(solution)/shard_map/all_to_all | solution.py:97
  106.5 24.1 %all-gather.14.cloned.1.call-done = bf16[768,768]{1,0:T(8,128)(2,1)} async-done(((bf16[24,768]{1,0:T(8,128)(2,1)}), bf16[768,768]{1,0:T(8,128)(2,1)}) %all-gather.14.cloned.1.call-update) | async-done | bytes 1179664 | tf_op jit(solution)/shard_map/all_gather | solution.py:75
  130.7 3.8 convolution_convert_fusion.2
  138.6 48.0 %all-gather.12.cloned.1.call-done = bf16[768,768]{1,0:T(8,128)(2,1)} async-done(((bf16[24,768]{1,0:T(8,128)(2,1)}), bf16[768,768]{1,0:T(8,128)(2,1)}) %all-gather.12.cloned.1.call-update) | async-done | bytes 1179664 | tf_op jit(solution)/shard_map/all_gather | solution.py:74
  186.6 3.1 add_convert_fusion.3
  191.4 2.9 reshape.313
  194.3 48.1 %all-gather.10.cloned.1.call-done = bf16[768,768]{1,0:T(8,128)(2,1)} async-done(((bf16[24,768]{1,0:T(8,128)(2,1)}), bf16[768,768]{1,0:T(8,128)(2,1)}) %all-gather.10.cloned.1.call-update) | async-done | bytes 1179664 | tf_op jit(solution)/shard_map/all_gather | solution.py:76
  242.3 4.3 add_convert_fusion.4
  246.6 2.6 copy.64
  249.2 3.9 reshape.312
  253.0 7.8 fusion.39
  260.8 12.9 %fusion.78 = (f32[4,12,256]{2,1,0:T(8,128)S(1)}, f32[4,12,256,256]{2,3,1,0:T(8,128)S(1)}) fusion(f32[4,12,256,256]{2,3,1,0:T(8,128)} %fusion.39, pred[4,256]{1,0:T(4,128)(4,1)S(1)} %get-tuple-element.137), kind=kOutput, calls=%fused_computation.163 | output fusion | flops 18874624 | bytes 25216000 | tf_op jit(solution)/shard_map/sub | solution.py:150
  274.9 3.4 copy-done.8
  281.2 16.9 %all-gather.16.cloned.1.call-done = bf16[768,768]{1,0:T(8,128)(2,1)} async-done(((bf16[24,768]{1,0:T(8,128)(2,1)}), bf16[768,768]{1,0:T(8,128)(2,1)}) %all-gather.16.cloned.1.call-update) | async-done | bytes 1179664 | tf_op jit(solution)/shard_map/all_gather | solution.py:77
  298.1 3.4 fusion.79
  303.8 59.7 %all-gather.18.cloned.1.call-done = bf16[768,3072]{1,0:T(8,128)(2,1)} async-done(((bf16[24,3072]{1,0:T(8,128)(2,1)}), bf16[768,3072]{1,0:T(8,128)(2,1)}) %all-gather.18.cloned.1.call-update) | async-done | bytes 4718608 | tf_op jit(solution)/shard_map/all_gather | solution.py:78
  363.4 38.1 %multiply_convert_fusion.1 = (bf16[1024,3072]{1,0:T(8,128)(2,1)}, f32[1024,3072]{1,0:T(8,128)}, f32[1024,3072]{1,0:T(8,128)}) fusion(f32[3072]{0:T(1024)S(1)} %copy-done.60, bf16[768,3072]{1,0:T(8,128)(2,1)} %all-gather.18.cloned.1.call-done, f32[1024,768]{1,0:T(8,128)} %copy-done.3, f32[768]{0:T(1024)S(1)} %copy-done.34, f32[768]{0:T(1024)S(1)} %copy-done.29, ...), kind=kOutput, calls=%fused_computation.7 | convolution fusion | flops 5043388416 | bytes 39348224 | tf_op jit(solution)/shard_map/dot_general | solution.py:165
  401.5 27.3 %all-gather.20.cloned.1.call-done = bf16[3072,768]{1,0:T(8,128)(2,1)} async-done(((bf16[96,768]{1,0:T(8,128)(2,1)}), bf16[3072,768]{1,0:T(8,128)(2,1)}) %all-gather.20.cloned.1.call-update) | async-done | bytes 4718608 | tf_op jit(solution)/shard_map/all_gather | solution.py:79
  428.8 9.3 fusion.80
  439.6 2.4 multiply_reduce_fusion.1
  442.0 3.7 convert_reduce_fusion.1
  445.8 7.8 fusion.68
  453.6 18.8 %convert_reduce_fusion = (f32[3072]{0:T(1024)S(1)}, bf16[1024,3072]{1,0:T(8,128)(2,1)}) fusion(f32[1024,3072]{1,0:T(8,128)} %get-tuple-element.132, bf16[3072,768]{1,0:T(8,128)(2,1)} %all-gather.20.cloned.1.call-done, f32[1024,768]{1,0:T(8,128)} %copy-done.15, f32[1024,3072]{1,0:T(8,128)} %get-tuple-element.152, f32[3072]{0:T(1024)S(1)} %copy-done.60), kind=kOutput, calls=%fused_computation.3 | convolution fusion | flops 4886098944 | bytes 39346176 | tf_op jit(solution)/shard_map/rb,ab->ra/dot_general | solution.py:36
  472.4 10.1 multiply_reduce_fusion.2
  483.9 2.8 fusion.65
  486.7 2.6 convolution_convert_fusion.1
  493.4 7.3 convert_reduce_fusion.3
  500.8 8.9 multiply_reduce_fusion
  509.7 6.9 multiply_convert_fusion
  521.6 2.9 fusion.87
  527.6 2.9 fusion.85
  530.5 2.9 fusion.86
  541.7 3.5 all-to-all-start.1
  545.3 11.0 fusion.81
  556.3 9.5 all-to-all-done.1
  573.0 4.5 convolution_bitcast_fusion
  578.8 43.5 %all-reduce = (f32[4,768]{1,0:T(4,128)}, f32[768]{0:T(1024)}, f32[768]{0:T(1024)}, f32[768]{0:T(1024)}, f32[768]{0:T(1024)}, /*index=5*/f32[768]{0:T(1024)}, f32...) all-reduce(f32[4,768]{1,0:T(4,128)S(1)} %convolution_bitcast_fusion, ...), channel_id=1, replica_groups=mesh['enc'=4,'dp'=8] {'enc','dp'}, use_global_device_ids=true, to_apply=%region_17.19 | all-reduce | flops 14592 | bytes 116736 | tf_op jit(solution)/shard_map/psum | solution.py:277
  623.3 4.9 convolution_convert_fusion
  628.2 476.7 %all-reduce.4.cloned.1.call-done = (f32[2048,768]{0,1:T(8,128)}, f32[768,768]{1,0:T(8,128)}, f32[768,768]{1,0:T(8,128)}, f32[768,768]{1,0:T(8,128)}, f32[768,768...) async-done(((f32[2048,768]{0,1:T(8,128)}, f32[768,768]{1,0:T(8,128)}, f32[768,768]{1,0:T(8,128)}, f32[768,768]{1,0:T(8,128)}, f32[768,768]{1,0:T(8,128)}, ...) | async-done | bytes 34603024 | tf_op jit(solution)/shard_map/psum | solution.py:277
  1104.9 6.6 copy.84
  1111.4 3.4 copy.126
  1121.2 9.3 copy.130
  1130.6 3.7 copy.131
  (228 shorter events, 63.3 us)
Async XLA Ops:
  7.2 65.4 %copy-start = (bf16[416,2048]{1,0:T(8,128)(2,1)S(1)}, bf16[416,2048]{1,0:T(8,128)(2,1)}, u32[]{:S(2)}) copy-start(bf16[416,2048]{1,0:T(8,128)(2,1)} %param.34) | copy-start | bytes 5111812
  7.2 65.4 %all-gather.8.cloned.1.call-start = ((), (), s32[]{:S(2)}) async-start(), calls=%async_computation.2 | async-start | bytes 3244032 | tf_op jit(solution)/shard_map/all_gather | solution.py:73
  7.9 122.7 %all-gather.14.cloned.1.call-start = ((), (), s32[]{:S(2)}) async-start(), calls=%async_computation.5 | async-start | bytes 1216512 | tf_op jit(solution)/shard_map/all_gather | solution.py:75
  8.7 177.9 %all-gather.12.cloned.1.call-start = ((), (), s32[]{:S(2)}) async-start(), calls=%async_computation.4 | async-start | bytes 1216512 | tf_op jit(solution)/shard_map/all_gather | solution.py:74
  9.4 232.9 %all-gather.10.cloned.1.call-start = ((), (), s32[]{:S(2)}) async-start(), calls=%async_computation.3 | async-start | bytes 1216512 | tf_op jit(solution)/shard_map/all_gather | solution.py:76
  10.0 288.1 %all-gather.16.cloned.1.call-start = ((), (), s32[]{:S(2)}) async-start(), calls=%async_computation.6 | async-start | bytes 1216512 | tf_op jit(solution)/shard_map/all_gather | solution.py:77
  10.6 352.9 %all-gather.18.cloned.1.call-start = ((), (), s32[]{:S(2)}) async-start(), calls=%async_computation.7 | async-start | bytes 4866048 | tf_op jit(solution)/shard_map/all_gather | solution.py:78
  11.2 64.8 %copy-start.38 = (bf16[4,768]{1,0:T(4,128)(2,1)S(1)}, bf16[4,768]{1,0:T(4,128)(2,1)}, u32[]{:S(2)}) copy-start(bf16[4,768]{1,0:T(4,128)(2,1)} %param.40) | copy-start | bytes 18436
  11.2 64.8 %copy-start.41 = (bf16[4,416]{1,0:T(4,128)(2,1)S(1)}, bf16[4,416]{1,0:T(4,128)(2,1)}, u32[]{:S(2)}) copy-start(bf16[4,416]{1,0:T(4,128)(2,1)} %param.35) | copy-start | bytes 9988
  11.2 64.8 %copy-start.47 = (f32[768]{0:T(1024)S(1)}, f32[768]{0:T(1024)}, u32[]{:S(2)}) copy-start(f32[768]{0:T(1024)} %param.41) | copy-start | bytes 9220
  76.5 7.8 copy-start.46
  76.5 7.8 copy-start.56
  79.5 24.9 %all-to-all-start = ((bf16[32,13,768]{2,1,0:T(8,128)(2,1)}), bf16[32,13,768]{2,1,0:T(8,128)(2,1)S(1)}, u32[]{:S(2)}, u32[]{:S(2)}) async-start(bf16[32,13,768]{2,1,0:T(8,128)(2,1)} %all_to_all.14), calls=%async_computation | async-start | bytes 1572864 | tf_op jit(solution)/shard_map/all_to_all | solution.py:97
  82.9 345.9 %all-gather.20.cloned.1.call-start = ((), (), s32[]{:S(2)}) async-start(), calls=%async_computation.8 | async-start | bytes 4866048 | tf_op jit(solution)/shard_map/all_gather | solution.py:79
  88.4 16.9 %copy-start.54 = (pred[512]{0:T(512)(128)(4,1)}, pred[512]{0:T(512)(128)(4,1)S(1)}, u32[]{:S(2)}) copy-start(pred[512]{0:T(512)(128)(4,1)S(1)} %select_compare_fusion) | copy-start | bytes 1540
  88.4 16.8 %copy-start.50 = (s32[416]{0:T(512)}, s32[416]{0:T(512)S(1)}, u32[]{:S(2)}) copy-start(s32[416]{0:T(512)S(1)} %fusion.52) | copy-start | bytes 4996
  91.6 13.6 %copy-start.52 = (s32[512]{0:T(512)}, s32[512]{0:T(512)S(1)}, u32[]{:S(2)}) copy-start(s32[512]{0:T(512)S(1)} %select_add_fusion) | copy-start | bytes 6148
  106.5 24.1 %copy-start.19 = (bf16[4,256,768]{2,1,0:T(8,128)(2,1)}, bf16[4,256,768]{2,1,0:T(8,128)(2,1)S(1)}, u32[]{:S(2)}) copy-start(bf16[4,256,768]{2,1,0:T(8,128)(2,1)S(1)} %pad_maximum_fusion) | copy-start | bytes 4718596
  134.5 52.1 %copy-start.61 = (f32[768]{0:T(1024)S(1)}, f32[768]{0:T(1024)}, u32[]{:S(2)}) copy-start(f32[768]{0:T(1024)} %param.45) | copy-start | bytes 9220
  189.7 52.6 %copy-start.62 = (f32[768]{0:T(1024)S(1)}, f32[768]{0:T(1024)}, u32[]{:S(2)}) copy-start(f32[768]{0:T(1024)} %param.48) | copy-start | bytes 9220
  194.2 58.8 %copy-start.5 = (bf16[4,256,12,64]{1,0,3,2:T(4,128)(2,1)}, bf16[4,256,12,64]{1,0,3,2:T(4,128)(2,1)S(1)}, u32[]{:S(2)}) copy-start(bf16[4,256,12,64]{1,0,3,2:T(4,128)(2,1)S(1)} %reshape.313) | copy-start | bytes 4718596
  260.8 12.9 %copy-start.22 = (bf16[4,256,12,64]{1,0,3,2:T(4,128)(2,1)S(1)}, bf16[4,256,12,64]{1,0,3,2:T(4,128)(2,1)}, u32[]{:S(2)}) copy-start(bf16[4,256,12,64]{1,0,3,2:T(4,128)(2,1)} %reshape.312) | copy-start | bytes 4718596
  273.7 4.8 copy-start.27
  278.5 19.6 %copy-start.20 = (bf16[4,256,768]{2,1,0:T(8,128)(2,1)S(1)}, bf16[4,256,768]{2,1,0:T(8,128)(2,1)}, u32[]{:S(2)}) copy-start(bf16[4,256,768]{2,1,0:T(8,128)(2,1)} %copy-done.19) | copy-start | bytes 4718596
  278.5 19.6 %copy-start.63 = (f32[768]{0:T(1024)S(1)}, f32[768]{0:T(1024)}, u32[]{:S(2)}) copy-start(f32[768]{0:T(1024)} %param.50) | copy-start | bytes 9220
  301.5 61.9 %copy-start.29 = (f32[768]{0:T(1024)S(1)}, f32[768]{0:T(1024)}, u32[]{:S(2)}) copy-start(f32[768]{0:T(1024)} %param.51) | copy-start | bytes 9220
  301.5 61.9 %copy-start.34 = (f32[768]{0:T(1024)S(1)}, f32[768]{0:T(1024)}, u32[]{:S(2)}) copy-start(f32[768]{0:T(1024)} %param.52) | copy-start | bytes 9220
  301.5 61.9 %copy-start.60 = (f32[3072]{0:T(1024)S(1)}, f32[3072]{0:T(1024)}, u32[]{:S(2)}) copy-start(f32[3072]{0:T(1024)} %param.54) | copy-start | bytes 36868
  303.7 125.1 %copy-start.64 = (f32[768]{0:T(1024)S(1)}, f32[768]{0:T(1024)}, u32[]{:S(2)}) copy-start(f32[768]{0:T(1024)} %param.56) | copy-start | bytes 9220
  439.6 6.2 slice-start.6
  445.8 7.8 copy-start.15
  453.6 18.8 %copy-start.4 = (f32[1024,768]{1,0:T(8,128)S(1)}, f32[1024,768]{1,0:T(8,128)}, u32[]{:S(2)}) copy-start(f32[1024,768]{1,0:T(8,128)} %copy-done.3) | copy-start | bytes 9437188
  493.4 7.3 copy-start.23
  493.4 7.4 copy-start.25
  493.4 16.3 %slice-start = ((s8[12582912]{0:T(1024)(128)(4,1)}), s8[4194304]{0:T(1024)(128)(4,1)S(1)}, s32[]{:S(2)}) async-start(s8[12582912]{0:T(1024)(128)(4,1)} %bitcast.136), calls=%async_computation.10 | async-start | bytes 8388608
  493.4 16.3 %slice-start.1 = ((s8[12582912]{0:T(1024)(128)(4,1)}), s8[4194304]{0:T(1024)(128)(4,1)S(1)}, s32[]{:S(2)}) async-start(s8[12582912]{0:T(1024)(128)(4,1)} %bitcast.136), calls=%async_computation.11 | async-start | bytes 8388608
  500.8 8.9 slice-start.2
  509.7 6.9 copy-start.6
  541.7 24.1 %all-to-all-start.1 = ((bf16[32,13,768]{2,1,0:T(8,128)(2,1)}), bf16[32,13,768]{2,1,0:T(8,128)(2,1)}, u32[]{:S(2)}, u32[]{:S(2)}) async-start(bf16[32,13,768]{2,1,0:T(8,128)(2,1)} %all_to_all.17), calls=%async_computation.1 | async-start | bytes 1572864 | tf_op jit(solution)/shard_map/all_to_all | solution.py:242
  545.2 20.6 %copy-start.31 = (f32[768]{0:T(1024)S(1)}, f32[768]{0:T(1024)}, u32[]{:S(2)}) copy-start(f32[768]{0:T(1024)} %param.42) | copy-start | bytes 9220
  545.3 24.5 %copy-start.33 = (f32[416]{0:T(512)S(1)}, f32[416]{0:T(512)}, u32[]{:S(2)}) copy-start(f32[416]{0:T(512)} %copy-done.32) | copy-start | bytes 4996
  545.3 24.5 %copy-start.37 = (f32[416]{0:T(512)S(1)}, f32[416]{0:T(512)}, u32[]{:S(2)}) copy-start(f32[416]{0:T(512)} %copy-done.36) | copy-start | bytes 4996
  545.3 559.6 %all-reduce.4.cloned.1.call-start = ((), (), s32[]{:S(2)}) async-start(), calls=%async_computation.9 | async-start | bytes 69206016 | tf_op jit(solution)/shard_map/psum | solution.py:277
  556.3 13.5 %copy-start.2 = (f32[416,768]{1,0:T(8,128)S(1)}, f32[416,768]{1,0:T(8,128)}, u32[]{:S(2)}) copy-start(f32[416,768]{1,0:T(8,128)} %copy-done.1) | copy-start | bytes 3833860
  577.6 44.8 %copy-start.39 = (bf16[4,768]{1,0:T(4,128)(2,1)S(1)}, bf16[4,768]{1,0:T(4,128)(2,1)}, u32[]{:S(2)}) copy-start(bf16[4,768]{1,0:T(4,128)(2,1)} %param.40) | copy-start | bytes 18436
  1119.8 10.7 slice-start.3
  1121.2 9.3 slice-start.4
  1121.2 9.3 slice-start.5
  (35 other events, 68.3 us)
Sparse Core Ops, SparseCore 0:
  10.9 61.6 all-gather.7
  75.5 55.1 all-gather.13
  133.6 52.9 all-gather.11
  189.3 52.9 all-gather.9
  245.1 52.9 all-gather.15
  300.8 62.5 all-gather.17
  366.3 62.4 all-gather.19
  577.7 527.0 all-reduce.3
where the time goes:
time: 1150 us; the launch traced here: 1140 us
  waiting for transfers between devices  788 us (69%)
  matrix products  173 us (15%)
  local copies, waits for them, and re-layouts  74.1 us (6%)
  blocking collectives  43.5 us (4%)
  other arithmetic  39.3 us (3%)
  between operations  16 us (1%)
    psum x1, waiting for transfers between devices, body(): lax.psum((grad_w_img, grad_w_box, grad_b_img, grad_g_reg, grad_beta_reg,...  477 us
    all_gather x1, waiting for transfers between devices, body(): lax.all_gather(w_img, ('enc', 'dp'), axis=0, tiled=True)  61.4 us
    all_gather x1, waiting for transfers between devices, body(): lax.all_gather(w_up, ('enc', 'dp'), axis=0, tiled=True)  59.7 us
    all_gather x1, waiting for transfers between devices, body(): lax.all_gather(w_value, ('enc', 'dp'), axis=0, tiled=True)  48.1 us
    all_gather x1, waiting for transfers between devices, body(): lax.all_gather(w_query, ('enc', 'dp'), axis=0, tiled=True)  48 us
    psum x1, blocking collectives, body(): lax.psum((grad_w_img, grad_w_box, grad_b_img, grad_g_reg, grad_beta_reg,...  43.5 us
    unnamed x158, local copies, waits for them, and re-layouts  43 us
    dot_general x7, matrix products, back_product(): jnp.einsum('rb,ab->ra', row_grad, weight, preferred_element_type=jnp.floa...  41 us
  transfers between devices with their start and end apart: 10, of which 10 were waited for; matrix products, arithmetic and copies ran while one was open for 11% of the time, Pallas kernels for 0%

commit v1 on v0

--- a/solution.py
+++ b/solution.py
@@ -274,30 +274,33 @@
         grad_b_down,
         grad_g_two,
         grad_beta_two,
-    ) = lax.psum(
-        (
-            grad_w_img,
-            grad_w_box,
-            grad_b_img,
-            grad_g_reg,
-            grad_beta_reg,
-            grad_w_query,
-            grad_b_query,
-            grad_w_key,
-            grad_w_value,
-            grad_b_value,
-            grad_w_out,
-            grad_b_out,
-            grad_g_one,
-            grad_beta_one,
-            grad_w_up,
-            grad_b_up,
-            grad_w_down,
-            grad_b_down,
-            grad_g_two,
-            grad_beta_two,
+    ) = jax.lax.psum(
+        jax.lax.psum(
+            (
+                grad_w_img,
+                grad_w_box,
+                grad_b_img,
+                grad_g_reg,
+                grad_beta_reg,
+                grad_w_query,
+                grad_b_query,
+                grad_w_key,
+                grad_w_value,
+                grad_b_value,
+                grad_w_out,
+                grad_b_out,
+                grad_g_one,
+                grad_beta_one,
+                grad_w_up,
+                grad_b_up,
+                grad_w_down,
+                grad_b_down,
+                grad_g_two,
+                grad_beta_two,
+            ),
+            axis_name="dp",
         ),
-        ("enc", "dp"),
+        axis_name="enc",
     )
     return (
         output,

time: 1150 us -> 2190 us (1.90)
  waiting for transfers between devices: 788 us -> 1820 us
    psum x1 -> x2, waiting for transfers between devices: 477 us -> 1510 us  [the longest x1 1090 us: body(): jax.lax.psum(jax.lax.psum((grad_w_img, grad_w_box, grad_b_img, grad_g_reg...]
    psum x1 -> x2, blocking collectives: 43.5 us -> 55.7 us  [the longest x1 30.9 us: body(): jax.lax.psum(jax.lax.psum((grad_w_img, grad_w_box, grad_b_img, grad_g_reg...]
  transfers between devices with their start and end apart: 10 -> 11, of which waited for: 10 -> 11; matrix products, arithmetic and copies ran while one was open for 11% -> 6% of each run, Pallas kernels for 0% -> 0%
where the time goes in v1:
time: 2190 us; the launch traced here: 2180 us
  waiting for transfers between devices  1820 us (83%)
  matrix products  172 us (8%)
  local copies, waits for them, and re-layouts  74.1 us (3%)
  blocking collectives  55.7 us (3%)
  other arithmetic  39.3 us (2%)
    psum x1, waiting for transfers between devices, body(): jax.lax.psum(jax.lax.psum((grad_w_img, grad_w_box, grad_b_img, grad_g_reg...  1090 us
    psum x1, waiting for transfers between devices, body(): jax.lax.psum((grad_w_img, grad_w_box, grad_b_img, grad_g_reg, grad_beta_r...  414 us
    all_gather x1, waiting for transfers between devices, body(): lax.all_gather(w_img, ('enc', 'dp'), axis=0, tiled=True)  61.4 us
    all_gather x1, waiting for transfers between devices, body(): lax.all_gather(w_up, ('enc', 'dp'), axis=0, tiled=True)  59.7 us
    all_gather x1, waiting for transfers between devices, body(): lax.all_gather(w_value, ('enc', 'dp'), axis=0, tiled=True)  48.1 us
    all_gather x1, waiting for transfers between devices, body(): lax.all_gather(w_query, ('enc', 'dp'), axis=0, tiled=True)  48 us
  transfers between devices with their start and end apart: 11, of which 11 were waited for; matrix products, arithmetic and copies ran while one was open for 6% of the time, Pallas kernels for 0%

profile of v1, /device:TPU:0, one launch (start us, length us, event | category | flops | bytes accessed | tf_op | source)
XLA Modules:
  0.0 2183.6 jit_solution(10767650444943801594)
XLA Ops:
  11.2 61.4 %all-gather.8.cloned.1.call-done = bf16[2048,768]{1,0:T(8,128)(2,1)} async-done(((bf16[64,768]{1,0:T(8,128)(2,1)}), bf16[2048,768]{1,0:T(8,128)(2,1)}) %all-gather.8.cloned.1.call-update) | async-done | bytes 3145744 | tf_op jit(solution)/shard_map/all_gather | solution.py:73
  72.6 3.4 fusion.82
  79.5 3.4 all-to-all-start
  85.8 2.6 select_compare_fusion
  89.0 2.6 select_add_fusion
  91.7 12.7 all-to-all-done
  106.5 24.1 %all-gather.14.cloned.1.call-done = bf16[768,768]{1,0:T(8,128)(2,1)} async-done(((bf16[24,768]{1,0:T(8,128)(2,1)}), bf16[768,768]{1,0:T(8,128)(2,1)}) %all-gather.14.cloned.1.call-update) | async-done | bytes 1179664 | tf_op jit(solution)/shard_map/all_gather | solution.py:75
  130.7 3.8 convolution_convert_fusion.2
  138.6 48.0 %all-gather.12.cloned.1.call-done = bf16[768,768]{1,0:T(8,128)(2,1)} async-done(((bf16[24,768]{1,0:T(8,128)(2,1)}), bf16[768,768]{1,0:T(8,128)(2,1)}) %all-gather.12.cloned.1.call-update) | async-done | bytes 1179664 | tf_op jit(solution)/shard_map/all_gather | solution.py:74
  186.6 3.1 add_convert_fusion.3
  191.4 2.9 reshape.313
  194.3 48.1 %all-gather.10.cloned.1.call-done = bf16[768,768]{1,0:T(8,128)(2,1)} async-done(((bf16[24,768]{1,0:T(8,128)(2,1)}), bf16[768,768]{1,0:T(8,128)(2,1)}) %all-gather.10.cloned.1.call-update) | async-done | bytes 1179664 | tf_op jit(solution)/shard_map/all_gather | solution.py:76
  242.3 4.3 add_convert_fusion.4
  249.2 3.9 reshape.312
  253.0 7.8 fusion.39
  260.8 12.9 fusion.78
  274.9 3.4 copy-done.8
  281.2 16.9 all-gather.16.cloned.1.call-done
  298.1 3.4 fusion.79
  303.7 59.7 %all-gather.18.cloned.1.call-done = bf16[768,3072]{1,0:T(8,128)(2,1)} async-done(((bf16[24,3072]{1,0:T(8,128)(2,1)}), bf16[768,3072]{1,0:T(8,128)(2,1)}) %all-gather.18.cloned.1.call-update) | async-done | bytes 4718608 | tf_op jit(solution)/shard_map/all_gather | solution.py:78
  363.4 38.1 %multiply_convert_fusion.1 = (bf16[1024,3072]{1,0:T(8,128)(2,1)}, f32[1024,3072]{1,0:T(8,128)}, f32[1024,3072]{1,0:T(8,128)}) fusion(f32[3072]{0:T(1024)S(1)} %copy-done.60, bf16[768,3072]{1,0:T(8,128)(2,1)} %all-gather.18.cloned.1.call-done, f32[1024,768]{1,0:T(8,128)} %copy-done.3, f32[768]{0:T(1024)S(1)} %copy-done.34, f32[768]{0:T(1024)S(1)} %copy-done.29, ...), kind=kOutput, calls=%fused_computation.7 | convolution fusion | flops 5043388416 | bytes 39348224 | tf_op jit(solution)/shard_map/dot_general | solution.py:165
  401.5 27.3 %all-gather.20.cloned.1.call-done = bf16[3072,768]{1,0:T(8,128)(2,1)} async-done(((bf16[96,768]{1,0:T(8,128)(2,1)}), bf16[3072,768]{1,0:T(8,128)(2,1)}) %all-gather.20.cloned.1.call-update) | async-done | bytes 4718608 | tf_op jit(solution)/shard_map/all_gather | solution.py:79
  428.8 9.3 fusion.80
  442.0 3.7 convert_reduce_fusion.1
  445.8 7.8 fusion.68
  453.6 18.8 convert_reduce_fusion
  472.4 10.1 multiply_reduce_fusion.2
  483.9 2.8 fusion.65
  486.7 2.6 convolution_convert_fusion.1
  493.4 7.3 convert_reduce_fusion.3
  500.8 8.9 multiply_reduce_fusion
  509.7 6.9 multiply_convert_fusion
  521.6 2.9 fusion.87
  527.6 2.9 fusion.85
  530.5 2.9 fusion.86
  541.7 3.5 all-to-all-start.1
  545.3 11.0 fusion.81
  556.3 9.5 all-to-all-done.1
  573.0 4.5 convolution_bitcast_fusion
  577.6 414.3 %all-reduce.7.cloned.1.call-done = (f32[2048,768]{0,1:T(8,128)}, f32[768,768]{1,0:T(8,128)}, f32[768,768]{1,0:T(8,128)}, f32[768,768]{1,0:T(8,128)}, f32[768,768...) async-done(((f32[2048,768]{0,1:T(8,128)}, f32[768,768]{1,0:T(8,128)}, f32[768,768]{1,0:T(8,128)}, f32[768,768]{1,0:T(8,128)}, f32[768,768]{1,0:T(8,128)}, ...) | async-done | bytes 34603024 | tf_op jit(solution)/shard_map/psum | solution.py:278
  993.2 24.8 %all-reduce = (f32[4,768]{1,0:T(4,128)S(1)}, f32[768]{0:T(1024)S(1)}, f32[768]{0:T(1024)S(1)}, f32[768]{0:T(1024)S(1)}, f32[768]{0:T(1024)S(1)}, /*index=5*/f32[...) all-reduce(f32[4,768]{1,0:T(4,128)S(1)} %convolution_bitcast_fusion, ...), channel_id=1, replica_groups=mesh['enc'=4,'dp'=8] {'dp'}, use_global_device_ids=true, to_apply=%region_18.20 | all-reduce | flops 14592 | bytes 116736 | tf_op jit(solution)/shard_map/psum | solution.py:278
  1018.1 30.9 %all-reduce.2 = (f32[4,768]{1,0:T(4,128)}, f32[768]{0:T(1024)}, f32[768]{0:T(1024)}, f32[768]{0:T(1024)}, f32[768]{0:T(1024)}, /*index=5*/f32[768]{0:T(1024)}, f...) all-reduce(f32[4,768]{1,0:T(4,128)S(1)} %get-tuple-element.105, ...), channel_id=1, replica_groups=mesh['enc'=4,'dp'=8] {'enc'}, use_global_device_ids=true, to_apply=%region_19.21 | all-reduce | flops 14592 | bytes 116736 | tf_op jit(solution)/shard_map/psum | solution.py:277
  1049.8 4.6 convolution_convert_fusion
  1054.5 1092.9 %all-reduce.9.cloned.1.call-done = (f32[2048,768]{0,1:T(8,128)}, f32[768,768]{1,0:T(8,128)}, f32[768,768]{1,0:T(8,128)}, f32[768,768]{1,0:T(8,128)}, f32[768,768...) async-done(((f32[2048,768]{0,1:T(8,128)}, f32[768,768]{1,0:T(8,128)}, f32[768,768]{1,0:T(8,128)}, f32[768,768]{1,0:T(8,128)}, f32[768,768]{1,0:T(8,128)}, ...) | async-done | bytes 34603024 | tf_op jit(solution)/shard_map/psum | solution.py:277
  2147.4 6.6 copy.84
  2153.9 3.4 copy.133
  2163.7 9.3 copy.137
  2173.1 3.7 copy.138
  (232 shorter events, 68.3 us)
Async XLA Ops:
  7.2 65.4 %copy-start = (bf16[416,2048]{1,0:T(8,128)(2,1)S(1)}, bf16[416,2048]{1,0:T(8,128)(2,1)}, u32[]{:S(2)}) copy-start(bf16[416,2048]{1,0:T(8,128)(2,1)} %param.34) | copy-start | bytes 5111812
  7.2 65.4 %all-gather.8.cloned.1.call-start = ((), (), s32[]{:S(2)}) async-start(), calls=%async_computation.2 | async-start | bytes 3244032 | tf_op jit(solution)/shard_map/all_gather | solution.py:73
  7.9 122.7 %all-gather.14.cloned.1.call-start = ((), (), s32[]{:S(2)}) async-start(), calls=%async_computation.5 | async-start | bytes 1216512 | tf_op jit(solution)/shard_map/all_gather | solution.py:75
  8.7 177.9 %all-gather.12.cloned.1.call-start = ((), (), s32[]{:S(2)}) async-start(), calls=%async_computation.4 | async-start | bytes 1216512 | tf_op jit(solution)/shard_map/all_gather | solution.py:74
  9.4 232.9 %all-gather.10.cloned.1.call-start = ((), (), s32[]{:S(2)}) async-start(), calls=%async_computation.3 | async-start | bytes 1216512 | tf_op jit(solution)/shard_map/all_gather | solution.py:76
  10.0 288.1 %all-gather.16.cloned.1.call-start = ((), (), s32[]{:S(2)}) async-start(), calls=%async_computation.6 | async-start | bytes 1216512 | tf_op jit(solution)/shard_map/all_gather | solution.py:77
  10.6 352.9 %all-gather.18.cloned.1.call-start = ((), (), s32[]{:S(2)}) async-start(), calls=%async_computation.7 | async-start | bytes 4866048 | tf_op jit(solution)/shard_map/all_gather | solution.py:78
  11.2 64.8 %copy-start.38 = (bf16[4,768]{1,0:T(4,128)(2,1)S(1)}, bf16[4,768]{1,0:T(4,128)(2,1)}, u32[]{:S(2)}) copy-start(bf16[4,768]{1,0:T(4,128)(2,1)} %param.40) | copy-start | bytes 18436
  11.2 64.8 %copy-start.41 = (bf16[4,416]{1,0:T(4,128)(2,1)S(1)}, bf16[4,416]{1,0:T(4,128)(2,1)}, u32[]{:S(2)}) copy-start(bf16[4,416]{1,0:T(4,128)(2,1)} %param.35) | copy-start | bytes 9988
  11.2 64.8 %copy-start.47 = (f32[768]{0:T(1024)S(1)}, f32[768]{0:T(1024)}, u32[]{:S(2)}) copy-start(f32[768]{0:T(1024)} %param.41) | copy-start | bytes 9220
  76.5 7.8 copy-start.46
  76.5 7.8 copy-start.56
  79.5 24.9 %all-to-all-start = ((bf16[32,13,768]{2,1,0:T(8,128)(2,1)}), bf16[32,13,768]{2,1,0:T(8,128)(2,1)S(1)}, u32[]{:S(2)}, u32[]{:S(2)}) async-start(bf16[32,13,768]{2,1,0:T(8,128)(2,1)} %all_to_all.14), calls=%async_computation | async-start | bytes 1572864 | tf_op jit(solution)/shard_map/all_to_all | solution.py:97
  82.9 345.9 %all-gather.20.cloned.1.call-start = ((), (), s32[]{:S(2)}) async-start(), calls=%async_computation.8 | async-start | bytes 4866048 | tf_op jit(solution)/shard_map/all_gather | solution.py:79
  88.4 16.9 copy-start.54
  88.4 16.8 copy-start.50
  91.6 13.6 copy-start.52
  106.5 24.1 %copy-start.19 = (bf16[4,256,768]{2,1,0:T(8,128)(2,1)}, bf16[4,256,768]{2,1,0:T(8,128)(2,1)S(1)}, u32[]{:S(2)}) copy-start(bf16[4,256,768]{2,1,0:T(8,128)(2,1)S(1)} %pad_maximum_fusion) | copy-start | bytes 4718596
  134.5 52.1 %copy-start.61 = (f32[768]{0:T(1024)S(1)}, f32[768]{0:T(1024)}, u32[]{:S(2)}) copy-start(f32[768]{0:T(1024)} %param.45) | copy-start | bytes 9220
  189.7 52.6 %copy-start.62 = (f32[768]{0:T(1024)S(1)}, f32[768]{0:T(1024)}, u32[]{:S(2)}) copy-start(f32[768]{0:T(1024)} %param.48) | copy-start | bytes 9220
  194.2 58.8 %copy-start.5 = (bf16[4,256,12,64]{1,0,3,2:T(4,128)(2,1)}, bf16[4,256,12,64]{1,0,3,2:T(4,128)(2,1)S(1)}, u32[]{:S(2)}) copy-start(bf16[4,256,12,64]{1,0,3,2:T(4,128)(2,1)S(1)} %reshape.313) | copy-start | bytes 4718596
  260.8 12.9 copy-start.22
  278.5 19.6 copy-start.20
  278.5 19.6 copy-start.63
  301.5 61.9 %copy-start.29 = (f32[768]{0:T(1024)S(1)}, f32[768]{0:T(1024)}, u32[]{:S(2)}) copy-start(f32[768]{0:T(1024)} %param.51) | copy-start | bytes 9220
  301.5 61.9 %copy-start.34 = (f32[768]{0:T(1024)S(1)}, f32[768]{0:T(1024)}, u32[]{:S(2)}) copy-start(f32[768]{0:T(1024)} %param.52) | copy-start | bytes 9220
  301.5 61.9 %copy-start.60 = (f32[3072]{0:T(1024)S(1)}, f32[3072]{0:T(1024)}, u32[]{:S(2)}) copy-start(f32[3072]{0:T(1024)} %param.54) | copy-start | bytes 36868
  303.7 125.1 %copy-start.64 = (f32[768]{0:T(1024)S(1)}, f32[768]{0:T(1024)}, u32[]{:S(2)}) copy-start(f32[768]{0:T(1024)} %param.56) | copy-start | bytes 9220
  439.6 6.2 slice-start.6
  445.8 7.8 copy-start.15
  453.6 18.8 copy-start.4
  493.4 7.3 copy-start.23
  493.4 7.4 copy-start.25
  493.4 16.3 slice-start
  493.4 16.3 slice-start.1
  500.8 8.9 slice-start.2
  509.7 6.9 copy-start.6
  541.7 24.1 %all-to-all-start.1 = ((bf16[32,13,768]{2,1,0:T(8,128)(2,1)}), bf16[32,13,768]{2,1,0:T(8,128)(2,1)}, u32[]{:S(2)}, u32[]{:S(2)}) async-start(bf16[32,13,768]{2,1,0:T(8,128)(2,1)} %all_to_all.17), calls=%async_computation.1 | async-start | bytes 1572864 | tf_op jit(solution)/shard_map/all_to_all | solution.py:242
  545.2 20.6 copy-start.31
  545.3 24.5 %copy-start.33 = (f32[416]{0:T(512)S(1)}, f32[416]{0:T(512)}, u32[]{:S(2)}) copy-start(f32[416]{0:T(512)} %copy-done.32) | copy-start | bytes 4996
  545.3 24.5 %copy-start.37 = (f32[416]{0:T(512)S(1)}, f32[416]{0:T(512)}, u32[]{:S(2)}) copy-start(f32[416]{0:T(512)} %copy-done.36) | copy-start | bytes 4996
  545.3 446.6 %all-reduce.7.cloned.1.call-start = ((), (), s32[]{:S(2)}) async-start(), calls=%async_computation.9 | async-start | bytes 69206016 | tf_op jit(solution)/shard_map/psum | solution.py:278
  556.3 13.5 copy-start.2
  577.6 1569.8 %all-reduce.9.cloned.1.call-start = ((), (), s32[]{:S(2)}) async-start(), calls=%async_computation.10 | async-start | bytes 69206016 | tf_op jit(solution)/shard_map/psum | solution.py:277
  991.9 57.0 %copy-start.39 = (bf16[4,768]{1,0:T(4,128)(2,1)S(1)}, bf16[4,768]{1,0:T(4,128)(2,1)}, u32[]{:S(2)}) copy-start(bf16[4,768]{1,0:T(4,128)(2,1)} %param.40) | copy-start | bytes 18436
  2162.3 10.7 slice-start.3
  2163.7 9.3 slice-start.4
  2163.7 9.3 slice-start.5
  (36 other events, 73.0 us)
Sparse Core Ops, SparseCore 0:
  10.9 61.6 all-gather.7
  75.5 55.1 all-gather.13
  133.6 52.9 all-gather.11
  189.3 52.9 all-gather.9
  245.1 52.9 all-gather.15
  300.8 62.5 all-gather.17
  366.3 62.4 all-gather.19
  577.7 414.1 all-reduce.6
  995.3 1151.9 all-reduce.8
